TPU v7x, 32 devices: a whole 2x2x4 slice. The times are simulated.
32 devices in a mesh: group: 2 (over x), src: 16 (over z, y, core).
Axes of the slice: x: 2, y: 2, z: 4, core: 2. Of those that a mesh axis runs over, the one named last changes fastest.
Arguments:
- rcv_points: float32 [3, 4096], P(None, ('group', 'src')), parts along dimension 1, may hold values from -1 to 1
- rcv_normals: float32 [3, 4096], P(None, ('group', 'src')), parts along dimension 1, may hold values from -4 to 4
- left_modes: float32 [8, 4096], P(None, ('group', 'src')), parts along dimension 1, may hold values from -5 to 5
- vertices: float32 [3, 2048], P(None, ('group', 'src')), parts along dimension 1, may hold values from -1 to 1
- connect: int32 [2, 4096], P(None, ('group', 'src')), parts along dimension 1, may hold values from 0 to 1023, as said below
- right_modes: float32 [8, 4096], P(None, ('group', 'src')), parts along dimension 1, may hold values from -0.125 to 0.125
- mode_weights: float32 [16], P('group'), parts along dimension 0, may hold values from 0.25 to 1
Outputs:
- rcv_grad: float32 [6, 4096], P(None, ('group', 'src')), parts along dimension 1
- vert_grad: float32 [3, 2048], P(None, ('group', 'src')), parts along dimension 1
There are 2 independent parts, one for each index of `group`. A program takes and returns all parts, laid end to end along the dimension named above; each array names one. Nothing has to cross between parts.
Inputs may be any that keep to these rules, and one draw needn't show every extreme that they name: `connect`: a panel's first vertex is one of the 64 vertices held at the same index of src as the panel, and its second vertex is the next vertex number.
All inputs are finite; a program needn't handle non-finite values.
Results may differ from a plain program's by a relative error of at most 0.0003.
Values sent between devices are 32-bit elements; how exact they have to be, the bound alone decides.
No kernel may reach another device: no remote copies, remote signals or barrier semaphores. Data moves between devices by JAX's collectives and lax.ppermute only.
A program may use at most 64 MiB of HBM per device.

v0:
```python
import math
import jax
import jax.numpy as jnp
from jax import lax
from jax.sharding import PartitionSpec as P

core_term = 0.05
inverse_four_pi = 0.25 / math.pi


def shifted(value, axis, steps):
    count = lax.axis_size(axis)
    leading, last = (max(0, -steps), min(count, count - steps))
    return lax.ppermute(value, axis, [(source, source + steps) for source in range(leading, last)])


def lift_points(raw):
    return jnp.stack([raw[0], raw[1], 0.5 + 0.2 * raw[2]])


def place_points(raw):
    return jnp.stack([raw[0], raw[1], 0.2 * raw[2]])


def tile_energy(points, normals, first_end, second_end, coefficient):
    rel_first = points[:, None, :] - first_end[:, :, None]
    rel_second = points[:, None, :] - second_end[:, :, None]
    segment = (second_end - first_end)[:, :, None]
    cross_x = rel_first[1] * rel_second[2] - rel_first[2] * rel_second[1]
    cross_y = rel_first[2] * rel_second[0] - rel_first[0] * rel_second[2]
    cross_z = rel_first[0] * rel_second[1] - rel_first[1] * rel_second[0]
    cross_sq = cross_x * cross_x + cross_y * cross_y + cross_z * cross_z
    dist_first = jnp.sqrt(jnp.sum(rel_first * rel_first, axis=0))
    dist_second = jnp.sqrt(jnp.sum(rel_second * rel_second, axis=0))
    along_term = jnp.sum(segment * (rel_first / dist_first - rel_second / dist_second), axis=0)
    span_sq = jnp.sum(segment * segment, axis=0)
    denominator = cross_sq + core_term * (span_sq + 1.0)
    normal_term = (
        normals[0][None, :] * cross_x
        + normals[1][None, :] * cross_y
        + normals[2][None, :] * cross_z
    )
    influence = inverse_four_pi * normal_term * along_term / denominator
    return jnp.sum(coefficient * influence)


def tile_gradients(points, normals, first_end, second_end, coefficient):
    return jax.grad(tile_energy, argnums=(0, 1, 2, 3))(
        points, normals, first_end, second_end, coefficient
    )


def on_device(rcv_points, rcv_normals, left_modes, vertices, connect, right_modes, mode_weights):
    own_count = vertices.shape[1]
    next_first = shifted(vertices[:, :1], "src", -1)
    extended = jnp.concatenate([vertices, next_first], axis=1)
    places = place_points(extended)
    base_vertex = lax.axis_index("src") * own_count
    local_first = connect[0] - base_vertex
    local_second = local_first + 1
    first_end = places[:, local_first]
    second_end = places[:, local_second]
    points = lift_points(rcv_points)
    chain_scale = jnp.array([1.0, 1.0, 0.2], dtype=jnp.float32)[:, None]
    weighted = right_modes * mode_weights[:, None]
    receiver_count = rcv_points.shape[1] * lax.axis_size("src")
    source_count = connect.shape[1]
    start_totals = (
        jnp.zeros((3, source_count), jnp.float32),
        jnp.zeros((3, source_count), jnp.float32),
        jnp.zeros((6, receiver_count), jnp.float32),
    )
    shard_points = lax.all_gather(points, "src", axis=1, tiled=True)
    shard_normals = lax.all_gather(rcv_normals, "src", axis=1, tiled=True)
    shard_left = lax.all_gather(left_modes, "src", axis=1, tiled=True)
    row_count = shard_points.shape[1]
    width_rows = math.gcd(row_count, 2048)

    def advance(number, inner):
        sum_first, sum_second, receiver_buffer = inner
        local_start = number * width_rows
        block_points = lax.dynamic_slice_in_dim(shard_points, local_start, width_rows, 1)
        block_normals = lax.dynamic_slice_in_dim(shard_normals, local_start, width_rows, 1)
        block_left = lax.dynamic_slice_in_dim(shard_left, local_start, width_rows, 1)
        coefficient = jnp.einsum("mj,mi->ji", weighted, block_left, precision=lax.Precision.HIGHEST)
        grads = tile_gradients(block_points, block_normals, first_end, second_end, coefficient)
        rows_out = jnp.concatenate([grads[0] * chain_scale, grads[1]], axis=0)
        receiver_buffer = lax.dynamic_update_slice_in_dim(receiver_buffer, rows_out, local_start, 1)
        return (sum_first + grads[2], sum_second + grads[3], receiver_buffer)

    sum_first, sum_second, receiver_buffer = lax.fori_loop(
        0, row_count // width_rows, advance, start_totals
    )
    rcv_grad = lax.psum_scatter(receiver_buffer, "src", scatter_dimension=1, tiled=True)
    vertex_partial = jnp.zeros((3, own_count + 1), jnp.float32)
    vertex_partial = (
        vertex_partial.at[:, local_first].add(sum_first).at[:, local_second].add(sum_second)
    )
    incoming = shifted(vertex_partial[:, own_count:], "src", 1)
    own_part = vertex_partial[:, :own_count]
    own_part = jnp.concatenate([own_part[:, :1] + incoming, own_part[:, 1:]], axis=1)
    vert_grad = own_part * chain_scale
    return (rcv_grad, vert_grad)


def solution(mesh):
    in_specs = (
        P(None, ("group", "src")),
        P(None, ("group", "src")),
        P(None, ("group", "src")),
        P(None, ("group", "src")),
        P(None, ("group", "src")),
        P(None, ("group", "src")),
        P("group"),
    )
    out_specs = (P(None, ("group", "src")), P(None, ("group", "src")))
    return jax.shard_map(
        on_device, mesh=mesh, in_specs=in_specs, out_specs=out_specs, check_vma=False
    )
```

profile of v0, /device:TPU:0, one launch (start us, length us, event | category | flops | bytes accessed | tf_op | source)
XLA Modules:
  0.0 154.4 jit_solution(849035136935577808)
XLA Ops:
  7.2 0.0 reduce-scatter.2.cloned.1.call-start
  7.2 1.3 collective-permute-start
  8.5 0.7 multiply_add_fusion.1
  9.2 0.7 slice.81
  9.9 23.8 %all_gather.10 = f32[3,2048]{1,0:T(4,128)S(1)} all-gather(f32[3,128]{1,0:T(4,128)S(1)} %pad_maximum_fusion.3), channel_id=1, replica_groups=mesh['group'=2,'src'=16] {'src'}, dimensions={1}, use_global_device_ids=true | all-gather | bytes 26112 | tf_op jit(solution)/shard_map/all_gather | solution.py:73
  33.7 17.7 %all_gather.9 = f32[3,2048]{1,0:T(4,128)S(1)} all-gather(f32[3,128]{1,0:T(4,128)} %param.9), channel_id=1, replica_groups=mesh['group'=2,'src'=16] {'src'}, dimensions={1}, use_global_device_ids=true | all-gather | bytes 26112 | tf_op jit(solution)/shard_map/all_gather | solution.py:74
  51.4 19.2 %all_gather.11 = f32[8,2048]{1,0:T(8,128)S(1)} all-gather(f32[8,128]{1,0:T(8,128)} %param.10), channel_id=1, replica_groups=mesh['group'=2,'src'=16] {'src'}, dimensions={1}, use_global_device_ids=true | all-gather | bytes 69632 | tf_op jit(solution)/shard_map/all_gather | solution.py:75
  70.6 0.7 fusion.24
  71.3 0.0 collective-permute-done
  71.3 0.8 pad_maximum_fusion.1
  72.1 0.1 copy.26
  72.2 0.6 gather_fusion.1
  72.9 0.1 copy.29
  72.9 0.7 gather_fusion
  73.6 0.1 copy.27
  73.7 0.8 fusion.15
  74.5 0.0 copy-start.2
  74.5 0.0 copy-start.3
  74.6 0.3 multiply_divide_fusion.1
  74.9 0.3 multiply_divide_fusion.2
  75.3 0.0 copy-done.2
  75.3 0.0 copy-done.3
  75.3 1.8 %divide_multiply_fusion.1 = (f32[128,2048]{1,0:T(8,128)S(1)}, f32[128,2048]{1,0:T(8,128)S(1)}, f32[128,2048]{1,0:T(8,128)S(1)}, f32[128,2048]{1,0:T(8,128)S(1)},...) fusion(f32[128]{0:T(128)S(1)} %add_multiply_fusion.2, f32[2048]{0:T(1024)S(1)} %bitcast.136, ...), kind=kOutput, calls=%fused_computation.109 | convolution fusion | flops 31196160 | bytes 13726240 | tf_op jit(solution)/shard_map/while/body/eval_jaxpr/mj,mi->ji/dot_general | solution.py:85
  77.1 2.5 %multiply_reduce_fusion = (f32[3,128]{1,0:T(4,128)S(1)}, f32[128,2048]{1,0:T(8,128)S(1)}, f32[128,2048]{1,0:T(8,128)S(1)}, f32[128,2048]{1,0:T(8,128)S(1)}) fusion(f32[128,2048]{1,0:T(8,128)S(1)} %get-tuple-element.62, f32[128,2048]{1,0:T(8,128)S(1)} %get-tuple-element.92, f32[3,128]{1,0:T(4,128)S(1)} %bitcast.127, f32[128,2048]{1,0:T(8,128)S(1)} %get-tuple-element.94, ...), kind=kLoop, calls=%fused_computation.36 | loop fusion | flops 12582528 | bytes 8419328 | tf_op jit(solution)/shard_map/while/body/eval_jaxpr/transpose(jvp())/reduce_sum | solution.py:35
  79.6 0.2 multiply_multiply_fusion.3
  79.8 0.2 multiply_multiply_fusion.1
  80.1 0.6 fusion.28
  80.6 2.0 %multiply_bitcast_fusion.5 = (f32[1,128,2048]{2,1,0:T(8,128)}, f32[128,2048]{1,0:T(8,128)}, f32[128,2048]{1,0:T(8,128)S(1)}) fusion(f32[3,128,2048]{2,1,0:T(8,128)S(1)} %get-tuple-element.95, f32[128,2048]{1,0:T(8,128)S(1)} %get-tuple-element.67, f32[128,2048]{1,0:T(8,128)S(1)} %get-tuple-element.54, f32[2048]{0:T(1024)S(1)} %broadcast_multiply_fusion.2, ...), kind=kLoop, calls=%fused_computation.57 | loop fusion | flops 2359296 | bytes 9445376 | tf_op jit(solution)/shard_map/while/body/eval_jaxpr/transpose(jvp())/broadcast_in_dim | solution.py:31
  82.6 2.2 %multiply_bitcast_fusion.3 = (f32[1,128,2048]{2,1,0:T(8,128)S(1)}, f32[128,2048]{1,0:T(8,128)}, f32[1,128,2048]{2,1,0:T(8,128)S(1)}, f32[128,2048]{1,0:T(8,128)}...) fusion(f32[3,128,2048]{2,1,0:T(8,128)S(1)} %get-tuple-element.95, f32[128,2048]{1,0:T(8,128)S(1)} %get-tuple-element.66, ...), kind=kLoop, calls=%fused_computation.55 | loop fusion | flops 5236736 | bytes 11575296 | tf_op jit(solution)/shard_map/while/body/eval_jaxpr/transpose(jvp())/broadcast_in_dim | solution.py:30
  84.9 4.8 %multiply_bitcast_fusion.11 = (f32[1,128,2048]{2,1,0:T(8,128)S(1)}, f32[1,128,2048]{2,1,0:T(8,128)S(1)}, f32[1,128,2048]{2,1,0:T(8,128)S(1)}, f32[1,128,2048]{2,...) fusion(f32[128,2048]{1,0:T(8,128)} %get-tuple-element.56, ...), kind=kLoop, calls=%fused_computation.65 | loop fusion | flops 3145728 | bytes 18874368 | tf_op jit(solution)/shard_map/while/body/eval_jaxpr/transpose(jvp())/broadcast_in_dim | solution.py:31
  89.7 0.0 copy-start
  89.7 3.4 %fusion.27 = (f32[3,128]{1,0:T(4,128)S(1)}, f32[3,2048]{1,0:T(4,128)S(1)}) fusion(f32[1,128,2048]{2,1,0:T(8,128)} %get-tuple-element.88, f32[1,128,2048]{2,1,0:T(8,128)S(1)} %get-tuple-element.70, f32[1,128,2048]{2,1,0:T(8,128)} %get-tuple-element.89, f32[1,128,2048]{2,1,0:T(8,128)S(1)} %get-tuple-element.58, f32[1,128,2048]{2,1,0:T(8,128)} %get-tuple-element.90, ...), kind=kLoop, calls=%fused_computation.111 | loop fusion | flops 11003520 | bytes 9490944 | tf_op jit(solution)/shard_map/while/body/eval_jaxpr/transpose(jvp())/reduce_sum | solution.py:26
  93.1 0.0 copy-done
  93.1 0.0 copy-start.1
  93.1 1.9 %fusion.26 = (f32[3,128]{1,0:T(4,128)S(1)}, f32[3,2048]{1,0:T(4,128)S(1)}) fusion(f32[1,128,2048]{2,1,0:T(8,128)S(1)} %get-tuple-element.84, f32[1,128,2048]{2,1,0:T(8,128)S(1)} %get-tuple-element.85, f32[1,128,2048]{2,1,0:T(8,128)S(1)} %get-tuple-element.86, f32[1,128,2048]{2,1,0:T(8,128)S(1)} %copy-done, f32[1,128,2048]{2,1,0:T(8,128)S(1)} %get-tuple-element.73, ...), kind=kLoop, calls=%fused_computation.110 | loop fusion | flops 11789952 | bytes 9490944 | tf_op jit(solution)/shard_map/while/body/eval_jaxpr/transpose(jvp())/reduce_sum | solution.py:27
  95.0 0.1 copy.31
  95.1 0.1 copy.30
  95.2 1.0 scatter_custom_fusion
  96.2 1.2 scatter_fusion
  97.5 0.0 copy-done.1
  97.5 0.1 add_multiply_fusion.1
  97.6 0.6 pad_maximum_fusion
  98.2 0.0 reduce-scatter.2.cloned.1.call-update
  98.3 2.2 %collective-permute-start.1 = (f32[3,1]{0,1:T(1,128)S(1)}, f32[3,1]{0,1:T(1,128)S(1)}, u32[]{:S(2)}, u32[]{:S(2)}) collective-permute-start(f32[3,1]{0,1:T(1,128)S(1)} %slice.108), channel_id=1, source_target_pairs={{0,1},{1,2},{2,3},{3,4},{4,5},{5,6},{6,7},{7,8},{8,9},{9,10},{10,1... | collective-permute-start | bytes 44 | tf_op jit(solution)/shard_map/ppermute | solution.py:14
  100.5 0.1 copy.33
  100.6 0.7 collective-permute-done.1
  101.3 0.1 copy.32
  101.4 0.7 maximum_multiply_fusion
  102.1 45.5 %reduce-scatter.2.cloned.1.call-done = f32[6,128]{1,0:T(8,128)} async-done(((f32[6,2048]{1,0:T(8,128)}), f32[6,128]{1,0:T(8,128)}) %reduce-scatter.2.cloned.1.call-update) | async-done | bytes 3088 | tf_op jit(solution)/shard_map/reduce_scatter | solution.py:94
  (16 shorter events, 0.2 us)
Async XLA Ops:
  7.2 140.4 %reduce-scatter.2.cloned.1.call-start = ((), (), s32[]{:S(2)}) async-start(), calls=%async_computation.1 | async-start | bytes 69632 | tf_op jit(solution)/shard_map/reduce_scatter | solution.py:94
  7.2 64.1 %collective-permute-start = (f32[3,1]{1,0:T(4,128)}, f32[3,1]{1,0:T(4,128)S(1)}, u32[]{:S(2)}, u32[]{:S(2)}) collective-permute-start(f32[3,1]{1,0:T(4,128)} %bitcast.141), channel_id=1, source_target_pairs={{1,0},{2,1},{3,2},{4,3},{5,4},{6,5},{7,6},{8,7},{9,8},{10,9},{11,1... | collective-permute-start | bytes 44 | tf_op jit(solution)/shard_map/ppermute | solution.py:14
  74.5 0.7 copy-start.2
  74.5 0.7 copy-start.3
  89.7 3.4 %copy-start = (f32[1,128,2048]{2,1,0:T(8,128)S(1)}, f32[1,128,2048]{2,1,0:T(8,128)}, u32[]{:S(2)}) copy-start(f32[1,128,2048]{2,1,0:T(8,128)} %get-tuple-element.87) | copy-start | bytes 3145732
  93.1 4.4 %copy-start.1 = (f32[3]{0:T(128)S(1)}, f32[3]{0:T(128)}, u32[]{:S(2)}) copy-start(f32[3]{0:T(128)} %constant.34.clone) | copy-start | bytes 40
  98.3 3.1 %collective-permute-start.1 = (f32[3,1]{0,1:T(1,128)S(1)}, f32[3,1]{0,1:T(1,128)S(1)}, u32[]{:S(2)}, u32[]{:S(2)}) collective-permute-start(f32[3,1]{0,1:T(1,128)S(1)} %slice.108), channel_id=1, source_target_pairs={{0,1},{1,2},{2,3},{3,4},{4,5},{5,6},{6,7},{7,8},{8,9},{9,10},{10,1... | collective-permute-start | bytes 44 | tf_op jit(solution)/shard_map/ppermute | solution.py:14
Sparse Core Ops, SparseCore 0:
  98.4 49.1 reduce-scatter.1
where the time goes:
time: 155 us; the launch traced here: 154 us
  blocking collectives  60.7 us (39%)
  waiting for transfers between devices  46.3 us (30%)
  other arithmetic  25.1 us (16%)
  between operations  14.3 us (9%)
  starting transfers between devices  3.57 us (2%)
  local copies, waits for them, and re-layouts  2.68 us (2%)
  matrix products  1.85 us (1%)
    reduce_scatter x1, waiting for transfers between devices, on_device(): lax.psum_scatter(receiver_buffer, 'src', scatter_dimension=1, tiled=True)  45.5 us
    all_gather x1, blocking collectives, on_device(): shard_points = lax.all_gather(points, 'src', axis=1, tiled=True)  23.8 us
    all_gather x1, blocking collectives, on_device(): shard_left = lax.all_gather(left_modes, 'src', axis=1, tiled=True)  19.2 us
    all_gather x1, blocking collectives, on_device(): shard_normals = lax.all_gather(rcv_normals, 'src', axis=1, tiled=True)  17.7 us
    broadcast_in_dim x2, other arithmetic, tile_energy(): cross_z = rel_first[0] * rel_second[1] - rel_first[1] * rel_second[0]  6.79 us
    ppermute x2, starting transfers between devices, shifted(): lax.ppermute(value, axis, [(source, source + steps) for source in range(l...  3.54 us
    reduce_sum x1, other arithmetic, tile_energy(): rel_first = points[:, None, :] - first_end[:, :, None]  3.41 us
  transfers between devices with their start and end apart: 3, of which 2 were waited for; matrix products, arithmetic and copies ran while one was open for 2% of the time, Pallas kernels for 0%

commit v1 on v0

--- a/solution.py
+++ b/solution.py
@@ -72,7 +72,16 @@
     )
     shard_points = lax.all_gather(points, "src", axis=1, tiled=True)
     shard_normals = lax.all_gather(rcv_normals, "src", axis=1, tiled=True)
-    shard_left = lax.all_gather(left_modes, "src", axis=1, tiled=True)
+    ways = lax.axis_size("src")
+    up = [(d, (d + 1) % ways) for d in range(ways)]
+    down = [(d, (d - 1) % ways) for d in range(ways)]
+    earlier, later = ([left_modes], [left_modes])
+    for _ in range(ways // 2):
+        earlier.append(lax.ppermute(earlier[-1], "src", up))
+    for _ in range((ways - 1) // 2):
+        later.append(lax.ppermute(later[-1], "src", down))
+    line = jnp.concatenate([*earlier[::-1], *later[1:]], axis=1)
+    shard_left = jnp.roll(line, (lax.axis_index("src") - ways // 2) * left_modes.shape[1], axis=1)
     row_count = shard_points.shape[1]
     width_rows = math.gcd(row_count, 2048)
 

time: 155 us -> 180 us (1.16)
  starting transfers between devices: 3.57 us -> 35 us
  blocking collectives: 60.7 us -> 37.8 us
  waiting for transfers between devices: 46.3 us -> 62.7 us
    ppermute x0 -> x15, starting transfers between devices: none -> 32.4 us  [the longest x7 31.5 us: on_device(): later.append(lax.ppermute(later[-1], 'src', down))]
    all_gather x1 -> x0, blocking collectives: 19.2 us -> none  [on_device(): shard_left = lax.all_gather(left_modes, 'src', axis=1, tiled=True)]
    ppermute x0 -> x15, waiting for transfers between devices: none -> 11.6 us  [the longest x7 6.21 us: on_device(): later.append(lax.ppermute(later[-1], 'src', down))]
    reduce_scatter x1, waiting for transfers between devices: 45.5 us -> 50.4 us  [on_device(): lax.psum_scatter(receiver_buffer, 'src', scatter_dimension=1, tiled=True)]
    all_gather x1, blocking collectives: 23.8 us -> 20 us  [on_device(): shard_points = lax.all_gather(points, 'src', axis=1, tiled=True)]
  transfers between devices with their start and end apart: 3 -> 18, of which waited for: 2 -> 9; matrix products, arithmetic and copies ran while one was open for 2% -> 4% of each run, Pallas kernels for 0% -> 0%
where the time goes in v1:
time: 180 us
  waiting for transfers between devices  62.7 us (35%)
  blocking collectives  37.8 us (21%)
  starting transfers between devices  35 us (19%)
  other arithmetic  25 us (14%)
  between operations  14.5 us (8%)
  local copies, waits for them, and re-layouts  2.77 us (2%)
  matrix products  1.87 us (1%)
    reduce_scatter x1, waiting for transfers between devices, on_device(): lax.psum_scatter(receiver_buffer, 'src', scatter_dimension=1, tiled=True)  50.4 us
    ppermute x7, starting transfers between devices, on_device(): later.append(lax.ppermute(later[-1], 'src', down))  31.5 us
    all_gather x1, blocking collectives, on_device(): shard_points = lax.all_gather(points, 'src', axis=1, tiled=True)  20 us
    all_gather x1, blocking collectives, on_device(): shard_normals = lax.all_gather(rcv_normals, 'src', axis=1, tiled=True)  17.7 us
    broadcast_in_dim x2, other arithmetic, tile_energy(): cross_z = rel_first[0] * rel_second[1] - rel_first[1] * rel_second[0]  6.8 us
    ppermute x7, waiting for transfers between devices, on_device(): later.append(lax.ppermute(later[-1], 'src', down))  6.21 us
    ppermute x8, waiting for transfers between devices, on_device(): earlier.append(lax.ppermute(earlier[-1], 'src', up))  5.41 us
  transfers between devices with their start and end apart: 18, of which 9 were waited for; matrix products, arithmetic and copies ran while one was open for 4% of the time, Pallas kernels for 0%

profile of v1, /device:TPU:0, one launch (start us, length us, event | category | flops | bytes accessed | tf_op | source)
XLA Modules:
  0.0 179.7 jit_solution(8626271008787293637)
XLA Ops:
  7.2 0.0 reduce-scatter.2.cloned.1.call-start
  7.2 0.5 collective-permute-start.1
  7.7 5.1 %collective-permute-start.9 = (f32[8,128]{1,0:T(8,128)}, f32[8,128]{1,0:T(8,128)S(1)}, u32[]{:S(2)}, u32[]{:S(2)}) collective-permute-start(f32[8,128]{1,0:T(8,128)} %param.10), channel_id=1, source_target_pairs={{0,15},{1,0},{2,1},{3,2},{4,3},{5,4},{6,5},{7,6},{8,7},{9,8},{10,9... | collective-permute-start | bytes 12296 | tf_op jit(solution)/shard_map/ppermute | solution.py:82
  12.8 1.3 collective-permute-start
  14.1 0.7 multiply_add_fusion.1
  14.8 0.7 slice.81
  15.5 20.0 %all_gather.7 = f32[3,2048]{1,0:T(4,128)S(1)} all-gather(f32[3,128]{1,0:T(4,128)S(1)} %pad_maximum_fusion.3), channel_id=1, replica_groups=mesh['group'=2,'src'=16] {'src'}, dimensions={1}, use_global_device_ids=true | all-gather | bytes 26112 | tf_op jit(solution)/shard_map/all_gather | solution.py:73
  35.5 17.7 %all_gather.6 = f32[3,2048]{1,0:T(4,128)S(1)} all-gather(f32[3,128]{1,0:T(4,128)} %param.9), channel_id=1, replica_groups=mesh['group'=2,'src'=16] {'src'}, dimensions={1}, use_global_device_ids=true | all-gather | bytes 26112 | tf_op jit(solution)/shard_map/all_gather | solution.py:74
  53.3 0.7 fusion.25
  54.0 0.0 collective-permute-done
  54.0 0.8 pad_maximum_fusion.1
  54.7 0.3 collective-permute-start.2
  55.1 5.4 %collective-permute-done.2 = f32[8,128]{1,0:T(8,128)S(1)} collective-permute-done((f32[8,128]{1,0:T(8,128)S(1)}, f32[8,128]{1,0:T(8,128)S(1)}, u32[]{:S(2)}, u32[]{:S(2)}) %collective-permute-start.2) | collective-permute-done | bytes 4128 | tf_op jit(solution)/shard_map/ppermute | solution.py:80
  60.5 0.0 collective-permute-start.3
  60.5 0.1 copy.26
  60.6 0.6 gather_fusion.1
  61.2 0.1 copy.29
  61.3 0.7 gather_fusion
  62.0 0.1 copy.27
  62.0 4.5 %collective-permute-start.10 = (f32[8,128]{1,0:T(8,128)S(1)}, f32[8,128]{1,0:T(8,128)S(1)}, u32[]{:S(2)}, u32[]{:S(2)}) collective-permute-start(f32[8,128]{1,0:T(8,128)S(1)} %collective-permute-done.9), channel_id=1, source_target_pairs={{0,15},{1,0},{2,1},{3,2},{4,3},{5,4},{6,5},{7,6},{8,7},{9,8},{10,9... | collective-permute-start | bytes 12296 | tf_op jit(solution)/shard_map/ppermute | solution.py:82
  66.5 0.8 fusion.15
  67.3 0.5 collective-permute-done.10
  67.8 4.4 %collective-permute-start.11 = (f32[8,128]{1,0:T(8,128)S(1)}, f32[8,128]{1,0:T(8,128)S(1)}, u32[]{:S(2)}, u32[]{:S(2)}) collective-permute-start(f32[8,128]{1,0:T(8,128)S(1)} %collective-permute-done.10), channel_id=1, source_target_pairs={{0,15},{1,0},{2,1},{3,2},{4,3},{5,4},{6,5},{7,6},{8,7},{9,8},{10,9... | collective-permute-start | bytes 12296 | tf_op jit(solution)/shard_map/ppermute | solution.py:82
  72.2 0.0 collective-permute-done.4
  72.2 0.0 copy-start.3
  72.3 0.0 copy-start.4
  72.3 0.3 multiply_divide_fusion.1
  72.6 0.9 collective-permute-done.11
  73.6 4.4 %collective-permute-start.12 = (f32[8,128]{1,0:T(8,128)S(1)}, f32[8,128]{1,0:T(8,128)S(1)}, u32[]{:S(2)}, u32[]{:S(2)}) collective-permute-start(f32[8,128]{1,0:T(8,128)S(1)} %collective-permute-done.11), channel_id=1, source_target_pairs={{0,15},{1,0},{2,1},{3,2},{4,3},{5,4},{6,5},{7,6},{8,7},{9,8},{10,9... | collective-permute-start | bytes 12296 | tf_op jit(solution)/shard_map/ppermute | solution.py:82
  78.0 0.0 collective-permute-done.5
  78.0 0.3 multiply_divide_fusion.2
  78.3 1.0 collective-permute-done.12
  79.3 4.4 %collective-permute-start.13 = (f32[8,128]{1,0:T(8,128)S(1)}, f32[8,128]{1,0:T(8,128)S(1)}, u32[]{:S(2)}, u32[]{:S(2)}) collective-permute-start(f32[8,128]{1,0:T(8,128)S(1)} %collective-permute-done.12), channel_id=1, source_target_pairs={{0,15},{1,0},{2,1},{3,2},{4,3},{5,4},{6,5},{7,6},{8,7},{9,8},{10,9... | collective-permute-start | bytes 12296 | tf_op jit(solution)/shard_map/ppermute | solution.py:82
  83.7 0.0 collective-permute-done.6
  83.7 1.3 collective-permute-done.13
  85.0 4.4 %collective-permute-start.14 = (f32[8,128]{1,0:T(8,128)S(1)}, f32[8,128]{1,0:T(8,128)S(1)}, u32[]{:S(2)}, u32[]{:S(2)}) collective-permute-start(f32[8,128]{1,0:T(8,128)S(1)} %collective-permute-done.13), channel_id=1, source_target_pairs={{0,15},{1,0},{2,1},{3,2},{4,3},{5,4},{6,5},{7,6},{8,7},{9,8},{10,9... | collective-permute-start | bytes 12296 | tf_op jit(solution)/shard_map/ppermute | solution.py:82
  89.4 0.0 collective-permute-done.7
  89.4 1.3 collective-permute-done.14
  90.7 4.4 %collective-permute-start.15 = (f32[8,128]{1,0:T(8,128)S(1)}, f32[8,128]{1,0:T(8,128)S(1)}, u32[]{:S(2)}, u32[]{:S(2)}) collective-permute-start(f32[8,128]{1,0:T(8,128)S(1)} %collective-permute-done.14), channel_id=1, source_target_pairs={{0,15},{1,0},{2,1},{3,2},{4,3},{5,4},{6,5},{7,6},{8,7},{9,8},{10,9... | collective-permute-start | bytes 12296 | tf_op jit(solution)/shard_map/ppermute | solution.py:82
  95.3 1.2 collective-permute-done.15
  96.6 1.9 %divide_multiply_fusion.1 = (f32[128,2048]{1,0:T(8,128)S(1)}, f32[128,2048]{1,0:T(8,128)S(1)}, f32[128,2048]{1,0:T(8,128)S(1)}, f32[128,2048]{1,0:T(8,128)S(1)},...) fusion(f32[128]{0:T(128)S(1)} %add_multiply_fusion.2, f32[2048]{0:T(1024)S(1)} %bitcast.135, ...), kind=kOutput, calls=%fused_computation.143 | convolution fusion | flops 31196160 | bytes 13726724 | tf_op jit(solution)/shard_map/while/body/eval_jaxpr/mj,mi->ji/dot_general | solution.py:94
  98.5 2.5 %multiply_reduce_fusion = (f32[3,128]{1,0:T(4,128)S(1)}, f32[128,2048]{1,0:T(8,128)S(1)}, f32[128,2048]{1,0:T(8,128)S(1)}, f32[128,2048]{1,0:T(8,128)S(1)}) fusion(f32[128,2048]{1,0:T(8,128)S(1)} %get-tuple-element.62, f32[128,2048]{1,0:T(8,128)S(1)} %get-tuple-element.92, f32[3,128]{1,0:T(4,128)S(1)} %bitcast.126, f32[128,2048]{1,0:T(8,128)S(1)} %get-tuple-element.94, ...), kind=kLoop, calls=%fused_computation.36 | loop fusion | flops 12582528 | bytes 8419328 | tf_op jit(solution)/shard_map/while/body/eval_jaxpr/transpose(jvp())/reduce_sum | solution.py:35
  101.0 0.2 multiply_multiply_fusion.3
  101.2 0.2 multiply_multiply_fusion.1
  101.4 0.5 fusion.30
  101.9 2.0 %multiply_bitcast_fusion.5 = (f32[1,128,2048]{2,1,0:T(8,128)}, f32[128,2048]{1,0:T(8,128)}, f32[128,2048]{1,0:T(8,128)S(1)}) fusion(f32[3,128,2048]{2,1,0:T(8,128)S(1)} %get-tuple-element.95, f32[128,2048]{1,0:T(8,128)S(1)} %get-tuple-element.67, f32[128,2048]{1,0:T(8,128)S(1)} %get-tuple-element.54, f32[2048]{0:T(1024)S(1)} %broadcast_multiply_fusion.2, ...), kind=kLoop, calls=%fused_computation.57 | loop fusion | flops 2359296 | bytes 9445376 | tf_op jit(solution)/shard_map/while/body/eval_jaxpr/transpose(jvp())/broadcast_in_dim | solution.py:31
  103.9 2.3 %multiply_bitcast_fusion.3 = (f32[1,128,2048]{2,1,0:T(8,128)S(1)}, f32[128,2048]{1,0:T(8,128)}, f32[1,128,2048]{2,1,0:T(8,128)S(1)}, f32[128,2048]{1,0:T(8,128)}...) fusion(f32[3,128,2048]{2,1,0:T(8,128)S(1)} %get-tuple-element.95, f32[128,2048]{1,0:T(8,128)S(1)} %get-tuple-element.66, ...), kind=kLoop, calls=%fused_computation.55 | loop fusion | flops 5236736 | bytes 11575296 | tf_op jit(solution)/shard_map/while/body/eval_jaxpr/transpose(jvp())/broadcast_in_dim | solution.py:30
  106.2 4.8 %multiply_bitcast_fusion.11 = (f32[1,128,2048]{2,1,0:T(8,128)S(1)}, f32[1,128,2048]{2,1,0:T(8,128)S(1)}, f32[1,128,2048]{2,1,0:T(8,128)S(1)}, f32[1,128,2048]{2,...) fusion(f32[128,2048]{1,0:T(8,128)} %get-tuple-element.56, ...), kind=kLoop, calls=%fused_computation.65 | loop fusion | flops 3145728 | bytes 18874368 | tf_op jit(solution)/shard_map/while/body/eval_jaxpr/transpose(jvp())/broadcast_in_dim | solution.py:31
  111.0 3.4 %fusion.29 = (f32[3,128]{1,0:T(4,128)S(1)}, f32[3,2048]{1,0:T(4,128)S(1)}) fusion(f32[1,128,2048]{2,1,0:T(8,128)} %get-tuple-element.88, f32[1,128,2048]{2,1,0:T(8,128)S(1)} %get-tuple-element.70, f32[1,128,2048]{2,1,0:T(8,128)} %get-tuple-element.89, f32[1,128,2048]{2,1,0:T(8,128)S(1)} %get-tuple-element.58, f32[1,128,2048]{2,1,0:T(8,128)} %get-tuple-element.90, ...), kind=kLoop, calls=%fused_computation.145 | loop fusion | flops 11003520 | bytes 9490944 | tf_op jit(solution)/shard_map/while/body/eval_jaxpr/transpose(jvp())/reduce_sum | solution.py:26
  114.4 0.0 copy-start.2
  114.4 1.9 %fusion.28 = (f32[3,128]{1,0:T(4,128)S(1)}, f32[3,2048]{1,0:T(4,128)S(1)}) fusion(f32[1,128,2048]{2,1,0:T(8,128)S(1)} %get-tuple-element.84, f32[1,128,2048]{2,1,0:T(8,128)S(1)} %get-tuple-element.85, f32[1,128,2048]{2,1,0:T(8,128)S(1)} %get-tuple-element.86, f32[1,128,2048]{2,1,0:T(8,128)S(1)} %copy-done, f32[1,128,2048]{2,1,0:T(8,128)S(1)} %get-tuple-element.73, ...), kind=kLoop, calls=%fused_computation.144 | loop fusion | flops 11789952 | bytes 9490944 | tf_op jit(solution)/shard_map/while/body/eval_jaxpr/transpose(jvp())/reduce_sum | solution.py:27
  116.3 0.1 copy.31
  116.4 0.1 copy.30
  116.5 1.0 scatter_custom_fusion
  117.5 1.2 scatter_fusion
  118.8 0.1 add_multiply_fusion.1
  118.9 0.6 pad_maximum_fusion
  119.6 0.0 reduce-scatter.2.cloned.1.call-update
  119.6 1.3 collective-permute-start.16
  120.9 0.1 copy.33
  121.0 0.7 collective-permute-done.16
  121.7 0.1 copy.32
  121.8 0.7 maximum_multiply_fusion
  122.4 50.4 %reduce-scatter.2.cloned.1.call-done = f32[6,128]{1,0:T(8,128)} async-done(((f32[6,2048]{1,0:T(8,128)}), f32[6,128]{1,0:T(8,128)}) %reduce-scatter.2.cloned.1.call-update) | async-done | bytes 3088 | tf_op jit(solution)/shard_map/reduce_scatter | solution.py:103
  (64 shorter events, 0.3 us)
Async XLA Ops:
  7.2 165.7 %reduce-scatter.2.cloned.1.call-start = ((), (), s32[]{:S(2)}) async-start(), calls=%async_computation.1 | async-start | bytes 69632 | tf_op jit(solution)/shard_map/reduce_scatter | solution.py:103
  7.2 47.5 %collective-permute-start.1 = (f32[8,128]{1,0:T(8,128)}, f32[8,128]{1,0:T(8,128)S(1)}, u32[]{:S(2)}, u32[]{:S(2)}) collective-permute-start(f32[8,128]{1,0:T(8,128)} %param.10), channel_id=1, source_target_pairs={{0,1},{1,2},{2,3},{3,4},{4,5},{5,6},{6,7},{7,8},{8,9},{9,10},{10,1... | collective-permute-start | bytes 12296 | tf_op jit(solution)/shard_map/ppermute | solution.py:80
  7.7 54.3 %collective-permute-start.9 = (f32[8,128]{1,0:T(8,128)}, f32[8,128]{1,0:T(8,128)S(1)}, u32[]{:S(2)}, u32[]{:S(2)}) collective-permute-start(f32[8,128]{1,0:T(8,128)} %param.10), channel_id=1, source_target_pairs={{0,15},{1,0},{2,1},{3,2},{4,3},{5,4},{6,5},{7,6},{8,7},{9,8},{10,9... | collective-permute-start | bytes 12296 | tf_op jit(solution)/shard_map/ppermute | solution.py:82
  12.8 41.2 %collective-permute-start = (f32[3,1]{1,0:T(4,128)}, f32[3,1]{1,0:T(4,128)S(1)}, u32[]{:S(2)}, u32[]{:S(2)}) collective-permute-start(f32[3,1]{1,0:T(4,128)} %bitcast.140), channel_id=1, source_target_pairs={{1,0},{2,1},{3,2},{4,3},{5,4},{6,5},{7,6},{8,7},{9,8},{10,9},{11,1... | collective-permute-start | bytes 44 | tf_op jit(solution)/shard_map/ppermute | solution.py:14
  54.7 5.7 %collective-permute-start.2 = (f32[8,128]{1,0:T(8,128)S(1)}, f32[8,128]{1,0:T(8,128)S(1)}, u32[]{:S(2)}, u32[]{:S(2)}) collective-permute-start(f32[8,128]{1,0:T(8,128)S(1)} %collective-permute-done.1), channel_id=1, source_target_pairs={{0,1},{1,2},{2,3},{3,4},{4,5},{5,6},{6,7},{7,8},{8,9},{9,10},{10,1... | collective-permute-start | bytes 12296 | tf_op jit(solution)/shard_map/ppermute | solution.py:80
  60.5 6.0 %collective-permute-start.3 = (f32[8,128]{1,0:T(8,128)S(1)}, f32[8,128]{1,0:T(8,128)S(1)}, u32[]{:S(2)}, u32[]{:S(2)}) collective-permute-start(f32[8,128]{1,0:T(8,128)S(1)} %collective-permute-done.2), channel_id=1, source_target_pairs={{0,1},{1,2},{2,3},{3,4},{4,5},{5,6},{6,7},{7,8},{8,9},{9,10},{10,1... | collective-permute-start | bytes 12296 | tf_op jit(solution)/shard_map/ppermute | solution.py:80
  62.0 5.8 %collective-permute-start.10 = (f32[8,128]{1,0:T(8,128)S(1)}, f32[8,128]{1,0:T(8,128)S(1)}, u32[]{:S(2)}, u32[]{:S(2)}) collective-permute-start(f32[8,128]{1,0:T(8,128)S(1)} %collective-permute-done.9), channel_id=1, source_target_pairs={{0,15},{1,0},{2,1},{3,2},{4,3},{5,4},{6,5},{7,6},{8,7},{9,8},{10,9... | collective-permute-start | bytes 12296 | tf_op jit(solution)/shard_map/ppermute | solution.py:82
  66.5 5.7 %collective-permute-start.4 = (f32[8,128]{1,0:T(8,128)S(1)}, f32[8,128]{1,0:T(8,128)S(1)}, u32[]{:S(2)}, u32[]{:S(2)}) collective-permute-start(f32[8,128]{1,0:T(8,128)S(1)} %collective-permute-done.3), channel_id=1, source_target_pairs={{0,1},{1,2},{2,3},{3,4},{4,5},{5,6},{6,7},{7,8},{8,9},{9,10},{10,1... | collective-permute-start | bytes 12296 | tf_op jit(solution)/shard_map/ppermute | solution.py:80
  67.8 5.7 %collective-permute-start.11 = (f32[8,128]{1,0:T(8,128)S(1)}, f32[8,128]{1,0:T(8,128)S(1)}, u32[]{:S(2)}, u32[]{:S(2)}) collective-permute-start(f32[8,128]{1,0:T(8,128)S(1)} %collective-permute-done.10), channel_id=1, source_target_pairs={{0,15},{1,0},{2,1},{3,2},{4,3},{5,4},{6,5},{7,6},{8,7},{9,8},{10,9... | collective-permute-start | bytes 12296 | tf_op jit(solution)/shard_map/ppermute | solution.py:82
  72.2 5.7 %collective-permute-start.5 = (f32[8,128]{1,0:T(8,128)S(1)}, f32[8,128]{1,0:T(8,128)S(1)}, u32[]{:S(2)}, u32[]{:S(2)}) collective-permute-start(f32[8,128]{1,0:T(8,128)S(1)} %collective-permute-done.4), channel_id=1, source_target_pairs={{0,1},{1,2},{2,3},{3,4},{4,5},{5,6},{6,7},{7,8},{8,9},{9,10},{10,1... | collective-permute-start | bytes 12296 | tf_op jit(solution)/shard_map/ppermute | solution.py:80
  72.2 23.0 %copy-start.1 = (f32[8,128]{1,0:T(8,128)S(1)}, f32[8,128]{1,0:T(8,128)}, u32[]{:S(2)}) copy-start(f32[8,128]{1,0:T(8,128)} %param.10) | copy-start | bytes 12292
  72.2 24.4 %copy-start.3 = (f32[8,128]{1,0:T(8,128)S(1)}, f32[8,128]{1,0:T(8,128)}, u32[]{:S(2)}) copy-start(f32[8,128]{1,0:T(8,128)} %param.13) | copy-start | bytes 12292
  72.3 24.4 %copy-start.4 = (f32[8]{0:T(128)S(1)}, f32[8]{0:T(128)}, u32[]{:S(2)}) copy-start(f32[8]{0:T(128)} %param.14) | copy-start | bytes 100
  73.6 5.7 %collective-permute-start.12 = (f32[8,128]{1,0:T(8,128)S(1)}, f32[8,128]{1,0:T(8,128)S(1)}, u32[]{:S(2)}, u32[]{:S(2)}) collective-permute-start(f32[8,128]{1,0:T(8,128)S(1)} %collective-permute-done.11), channel_id=1, source_target_pairs={{0,15},{1,0},{2,1},{3,2},{4,3},{5,4},{6,5},{7,6},{8,7},{9,8},{10,9... | collective-permute-start | bytes 12296 | tf_op jit(solution)/shard_map/ppermute | solution.py:82
  78.0 5.7 %collective-permute-start.6 = (f32[8,128]{1,0:T(8,128)S(1)}, f32[8,128]{1,0:T(8,128)S(1)}, u32[]{:S(2)}, u32[]{:S(2)}) collective-permute-start(f32[8,128]{1,0:T(8,128)S(1)} %collective-permute-done.5), channel_id=1, source_target_pairs={{0,1},{1,2},{2,3},{3,4},{4,5},{5,6},{6,7},{7,8},{8,9},{9,10},{10,1... | collective-permute-start | bytes 12296 | tf_op jit(solution)/shard_map/ppermute | solution.py:80
  79.3 5.7 %collective-permute-start.13 = (f32[8,128]{1,0:T(8,128)S(1)}, f32[8,128]{1,0:T(8,128)S(1)}, u32[]{:S(2)}, u32[]{:S(2)}) collective-permute-start(f32[8,128]{1,0:T(8,128)S(1)} %collective-permute-done.12), channel_id=1, source_target_pairs={{0,15},{1,0},{2,1},{3,2},{4,3},{5,4},{6,5},{7,6},{8,7},{9,8},{10,9... | collective-permute-start | bytes 12296 | tf_op jit(solution)/shard_map/ppermute | solution.py:82
  83.7 5.7 %collective-permute-start.7 = (f32[8,128]{1,0:T(8,128)S(1)}, f32[8,128]{1,0:T(8,128)S(1)}, u32[]{:S(2)}, u32[]{:S(2)}) collective-permute-start(f32[8,128]{1,0:T(8,128)S(1)} %collective-permute-done.6), channel_id=1, source_target_pairs={{0,1},{1,2},{2,3},{3,4},{4,5},{5,6},{6,7},{7,8},{8,9},{9,10},{10,1... | collective-permute-start | bytes 12296 | tf_op jit(solution)/shard_map/ppermute | solution.py:80
  85.0 5.7 %collective-permute-start.14 = (f32[8,128]{1,0:T(8,128)S(1)}, f32[8,128]{1,0:T(8,128)S(1)}, u32[]{:S(2)}, u32[]{:S(2)}) collective-permute-start(f32[8,128]{1,0:T(8,128)S(1)} %collective-permute-done.13), channel_id=1, source_target_pairs={{0,15},{1,0},{2,1},{3,2},{4,3},{5,4},{6,5},{7,6},{8,7},{9,8},{10,9... | collective-permute-start | bytes 12296 | tf_op jit(solution)/shard_map/ppermute | solution.py:82
  89.4 5.7 %collective-permute-start.8 = (f32[8,128]{1,0:T(8,128)S(1)}, f32[8,128]{1,0:T(8,128)S(1)}, u32[]{:S(2)}, u32[]{:S(2)}) collective-permute-start(f32[8,128]{1,0:T(8,128)S(1)} %collective-permute-done.7), channel_id=1, source_target_pairs={{0,1},{1,2},{2,3},{3,4},{4,5},{5,6},{6,7},{7,8},{8,9},{9,10},{10,1... | collective-permute-start | bytes 12296 | tf_op jit(solution)/shard_map/ppermute | solution.py:80
  90.7 5.7 %collective-permute-start.15 = (f32[8,128]{1,0:T(8,128)S(1)}, f32[8,128]{1,0:T(8,128)S(1)}, u32[]{:S(2)}, u32[]{:S(2)}) collective-permute-start(f32[8,128]{1,0:T(8,128)S(1)} %collective-permute-done.14), channel_id=1, source_target_pairs={{0,15},{1,0},{2,1},{3,2},{4,3},{5,4},{6,5},{7,6},{8,7},{9,8},{10,9... | collective-permute-start | bytes 12296 | tf_op jit(solution)/shard_map/ppermute | solution.py:82
  111.0 3.4 %copy-start = (f32[1,128,2048]{2,1,0:T(8,128)S(1)}, f32[1,128,2048]{2,1,0:T(8,128)}, u32[]{:S(2)}) copy-start(f32[1,128,2048]{2,1,0:T(8,128)} %get-tuple-element.87) | copy-start | bytes 3145732
  114.4 4.4 %copy-start.2 = (f32[3]{0:T(128)S(1)}, f32[3]{0:T(128)}, u32[]{:S(2)}) copy-start(f32[3]{0:T(128)} %constant.75.clone) | copy-start | bytes 40
  119.6 2.1 %collective-permute-start.16 = (f32[3,1]{0,1:T(1,128)S(1)}, f32[3,1]{0,1:T(1,128)S(1)}, u32[]{:S(2)}, u32[]{:S(2)}) collective-permute-start(f32[3,1]{0,1:T(1,128)S(1)} %slice.108), channel_id=1, source_target_pairs={{0,1},{1,2},{2,3},{3,4},{4,5},{5,6},{6,7},{7,8},{8,9},{9,10},{10,1... | collective-permute-start | bytes 44 | tf_op jit(solution)/shard_map/ppermute | solution.py:14
Sparse Core Ops, SparseCore 0:
  119.7 53.0 reduce-scatter.1
